TPU v7x, 32 devices: a whole 2x2x4 slice. The times are simulated.
32 devices in a mesh: groups: 2 (over x), expo: 8 (over z, y), sky: 2 (over core).
Axes of the slice: x: 2, y: 2, z: 4, core: 2. Of those that a mesh axis runs over, the one named last changes fastest.
Arguments:
- exposures: bfloat16 [384, 256, 512], P(('groups', 'expo'), 'sky'), parts along dimension 0, may hold values from -8 to 8
- slot_ids: int32 [16, 24], P('groups'), parts along dimension 0, may hold values from 0 to 128, as said below
- row_range: int32 [256, 2], P('groups'), parts along dimension 0, may hold values from 1 to 256, as said below
- bad_bands: int32 [256, 4], P('groups'), parts along dimension 0, may hold values 0 or 1
- kernel_choice: int32 [256, 4], P('groups'), parts along dimension 0, may hold values from 0 to 9
- flux_scale: float32 [256], P('groups'), parts along dimension 0, may hold values from 0.25 to 4
- vert_taps: bfloat16 [20, 21], P('groups'), parts along dimension 0, may hold values from -0.6 to 1.6
- horiz_taps: bfloat16 [20, 21], P('groups'), parts along dimension 0, may hold values from -0.6 to 1.6
Outputs:
- coadd_plane: float32 [4, 128, 512], P(('groups', 'sky'), 'expo'), parts along dimension 0
- rejected_count: int32 [4, 128, 512], P(('groups', 'sky'), 'expo'), parts along dimension 0
There are 2 independent parts, one for each index of `groups`. A program takes and returns all parts, laid end to end along the dimension named above; each array names one. Nothing has to cross between parts.
Inputs may be any that keep to these rules, and one draw needn't show every extreme that they name: `slot_ids`: each exposure number below 128 stands in exactly one slot; in each row the occupied slots come first and the others hold 128; a row has 8 to 24 occupied slots, and some row has all 24. `row_range`: column 0 is below 128 and column 1 is at least 128 and above column 0.
All inputs are finite; a program needn't handle non-finite values.
Results may differ from a plain program's by a relative error of at most 0.008.
Values may be sent and summed in bfloat16 or wider, within the bound.
A program may use at most 128 MiB of HBM per device.

v0:
```python
import functools

import jax
import jax.numpy as jnp
from jax import lax
from jax.experimental import pallas as pl
from jax.experimental.pallas import tpu as pltpu
from jax.sharding import PartitionSpec as P

BAND_COLS = 128
TAPS = 21
REJECT = 4
MIN_VALID = 12


SENTINEL = 1e30
HIGHEST = lax.Precision.HIGHEST


def padded_2(cells, sides, width):
    for axis, dim in sides:
        count = lax.axis_size(axis)
        ends = count - 1
        head = lax.slice_in_dim(cells, 0, width, axis=dim)
        tail = lax.slice_in_dim(cells, cells.shape[dim] - width, cells.shape[dim], axis=dim)
        cells = jnp.concatenate(
            [
                lax.ppermute(tail, axis, [(i, (i + 1) % count) for i in range(ends)]),
                cells,
                lax.ppermute(head, axis, [((i + 1) % count, i) for i in range(ends)]),
            ],
            axis=dim,
        )
    return cells


def shift_table(outputs, taps):
    out_index = jnp.arange(outputs, dtype=jnp.int32)[None, :, None]
    in_index = jnp.arange(outputs + taps - 1, dtype=jnp.int32)[None, None, :]
    offsets = jnp.arange(taps, dtype=jnp.int32)[:, None, None]
    return (in_index - out_index == offsets).astype(jnp.bfloat16)


def compare_pair(entries, first_place, second_place):
    larger = jnp.maximum(entries[first_place], entries[second_place])
    smaller = jnp.minimum(entries[first_place], entries[second_place])
    entries[first_place] = larger
    entries[second_place] = smaller


def leading_four(values):
    grouped = values.reshape((values.shape[0] // 4, 4) + values.shape[1:])
    entries = [grouped[:, position] for position in range(4)]
    for first_place, second_place in ((0, 1), (2, 3), (0, 2), (1, 3), (1, 2)):
        compare_pair(entries, first_place, second_place)
    while entries[0].shape[0] > 1:
        if entries[0].shape[0] % 2:
            entries = [
                jnp.concatenate(
                    [member, jnp.full((1,) + member.shape[1:], -SENTINEL, member.dtype)], 0
                )
                for member in entries
            ]
        middle = entries[0].shape[0] // 2
        merged = [
            jnp.maximum(entries[position][:middle], entries[3 - position][middle:])
            for position in range(4)
        ]
        for first_place, second_place in ((0, 2), (1, 3), (0, 1), (2, 3)):
            compare_pair(merged, first_place, second_place)
        entries = merged
    return jnp.concatenate(entries, 0)


def usable_mask(slot_list, first_row, row_count, row_range, bad_bands, exposures_total):
    lookup = jnp.minimum(slot_list, exposures_total - 1)
    picker = (lookup[:, None] == jnp.arange(exposures_total, dtype=jnp.int32)[None, :]).astype(
        jnp.float32
    )
    bounds = jnp.dot(picker, row_range.astype(jnp.float32), precision=HIGHEST)
    flagged = jnp.dot(picker, bad_bands.astype(jnp.float32), precision=HIGHEST)
    row_place = (first_row + jnp.arange(row_count, dtype=jnp.int32)).astype(jnp.float32)
    row_fine = (
        (row_place[None, :] >= bounds[:, 0:1])
        & (row_place[None, :] < bounds[:, 1:2])
        & (slot_list < exposures_total)[:, None]
    )
    column_fine = jnp.repeat(flagged < 0.5, BAND_COLS, axis=1)
    return row_fine[:, :, None] & column_fine[:, None, :]


def usable_count(first_row, row_count, row_range, bad_bands):
    row_place = (first_row + jnp.arange(row_count, dtype=jnp.int32)).astype(jnp.float32)
    bounds = row_range.astype(jnp.float32)
    covered = (
        (row_place[None, :] >= bounds[:, 0:1]) & (row_place[None, :] < bounds[:, 1:2])
    ).astype(jnp.float32)
    clean = (bad_bands == 0).astype(jnp.float32)
    per_band = jnp.dot(covered.T, clean, precision=HIGHEST)
    return jnp.repeat(per_band, BAND_COLS, axis=1).astype(jnp.int32)


def finish_pixels(grand_total, top_sum, bottom_sum, cover_count, exposures_total):
    clipped = cover_count >= MIN_VALID
    used_count = jnp.where(clipped, cover_count - 2 * REJECT, cover_count)
    kept_sum = jnp.where(clipped, grand_total - top_sum - bottom_sum, grand_total)
    coadd_plane = kept_sum / jnp.maximum(used_count, 1).astype(jnp.float32)
    return (coadd_plane, exposures_total - used_count)


def general_shards(
    exposures, slot_ids, row_range, bad_bands, kernel_choice, flux_scale, vert_taps, horiz_taps
):
    slot_count, row_dev, columns = exposures.shape
    exposures_total = flux_scale.shape[0]
    kernels = vert_taps.shape[0]
    margin = TAPS // 2
    band_count = columns // BAND_COLS
    expo_size = lax.axis_size("expo")
    expo_place = lax.axis_index("expo")
    sky_place = lax.axis_index("sky")
    negative_fill = jnp.asarray(-SENTINEL, jnp.bfloat16)
    own_slots = lax.dynamic_index_in_dim(slot_ids, expo_place, 0, keepdims=False)
    own_lookup = jnp.minimum(own_slots, exposures_total - 1)
    picker = (own_lookup[:, None] == jnp.arange(exposures_total, dtype=jnp.int32)[None, :]).astype(
        jnp.float32
    )
    chosen = jnp.dot(picker, kernel_choice.astype(jnp.float32), precision=HIGHEST)
    selector = (chosen[:, :, None] == jnp.arange(kernels, dtype=jnp.float32)[None, None, :]).astype(
        jnp.bfloat16
    )
    factor = jnp.dot(picker, flux_scale, precision=HIGHEST)
    block_rows = min(row_dev, 128)
    vertical_bank = jnp.einsum(
        "kt,tij->kij", vert_taps, shift_table(block_rows, TAPS), preferred_element_type=jnp.float32
    ).astype(jnp.bfloat16)
    vertical_pick = jnp.einsum(
        "sbk,kij->sbij", selector, vertical_bank, preferred_element_type=jnp.float32
    ).astype(jnp.bfloat16)
    widened = padded_2(exposures, (("sky", 1),), margin)
    widened = widened.reshape(slot_count, row_dev + 2 * margin, band_count, BAND_COLS)
    vertical_blocks = jnp.einsum(
        "sbij,sjbc->sibc", vertical_pick, widened, preferred_element_type=jnp.float32
    )
    vertical = vertical_blocks.astype(jnp.bfloat16).reshape(slot_count, row_dev, columns)
    horizontal_bank = jnp.einsum(
        "kt,tcj->kjc", horiz_taps, shift_table(BAND_COLS, TAPS), preferred_element_type=jnp.float32
    ).astype(jnp.bfloat16)
    horizontal_pick = jnp.einsum(
        "sbk,kjc->sbjc", selector, horizontal_bank, preferred_element_type=jnp.float32
    ).astype(jnp.bfloat16)
    padded = jnp.pad(vertical, ((0, 0), (0, 0), (margin, margin)))
    strips = jnp.stack(
        [
            padded[:, :, band_number * BAND_COLS : band_number * BAND_COLS + BAND_COLS + 2 * margin]
            for band_number in range(band_count)
        ],
        2,
    )
    filtered = jnp.einsum(
        "srbj,sbjc->srbc", strips, horizontal_pick, preferred_element_type=jnp.float32
    )
    planes = (filtered.reshape(slot_count, row_dev, columns) * factor[:, None, None]).astype(
        jnp.bfloat16
    )
    rows_out = row_dev // expo_size
    first_row = sky_place * row_dev + expo_place * rows_out
    cover_count = usable_count(first_row, rows_out, row_range, bad_bands)
    own_usable = usable_mask(
        own_slots, sky_place * row_dev, row_dev, row_range, bad_bands, exposures_total
    )
    partial_total = jnp.sum(
        jnp.where(own_usable, planes, jnp.zeros((), jnp.bfloat16)), axis=0, dtype=jnp.float32
    )[None]
    own_high = leading_four(jnp.where(own_usable, planes, negative_fill).reshape(slot_count, -1))
    own_low = leading_four(jnp.where(own_usable, -planes, negative_fill).reshape(slot_count, -1))
    extremes = jnp.concatenate([own_high, own_low], 0).reshape(8, row_dev, columns)
    received = lax.all_to_all(partial_total, "expo", split_axis=1, concat_axis=0, tiled=True)
    grand_total = jnp.sum(received, axis=0)
    arrived = lax.all_to_all(extremes, "expo", split_axis=1, concat_axis=0, tiled=True)
    senders = arrived.shape[0] // 8
    out_rows = arrived.shape[1]
    out_cols = arrived.shape[2]
    grouped = arrived.reshape(senders, 8, out_rows * out_cols)
    best_high = leading_four(grouped[:, :4].reshape(senders * 4, out_rows * out_cols))
    best_low = leading_four(grouped[:, 4:].reshape(senders * 4, out_rows * out_cols))
    high_sum = jnp.sum(best_high.astype(jnp.float32), axis=0).reshape(out_rows, out_cols)
    low_sum = -jnp.sum(best_low.astype(jnp.float32), axis=0).reshape(out_rows, out_cols)
    coadd_plane, rejected_count = finish_pixels(
        grand_total, high_sum, low_sum, cover_count, exposures_total
    )
    return (coadd_plane[None], rejected_count[None])


LANES = 128
FILL = 2.0**100
HALO = 16
UNROLL = 4
SORT_FOUR = ((0, 1), (2, 3), (0, 2), (1, 3), (1, 2))
SORT_BITONIC = ((0, 2), (1, 3), (0, 1), (2, 3))


def exchange(entries, places, first, second):
    for a, b in places:
        entries[a], entries[b] = first(entries[a], entries[b]), second(entries[a], entries[b])
    return entries


def merge_four(left, right, first, second, ordered=True):
    merged = [first(left[i], right[3 - i]) for i in range(4)]
    if ordered:
        exchange(merged, SORT_BITONIC, first, second)
    return merged


def flip_bit(place, bit):
    weight = 1 << bit
    return place + weight * (1 - 2 * ((place // weight) % 2))


def bit_order(band, steps):
    order = list(range(steps))
    if steps > 1 and band % 4 == 1:
        order[0], order[1] = order[1], order[0]
    return order


def flip_mask(place, mask, order):
    for position, bit in enumerate(order):
        if mask >> position & 1:
            place = flip_bit(place, bit)
    return place


def low_bit(mask, steps):
    for position in range(steps):
        if mask >> position & 1:
            return position
    return steps


def multiples(level, steps):
    masks = range(0, 1 << steps, 1 << level)
    return sorted(masks, key=lambda mask: -int(format(mask, f"0{steps}b")[::-1], 2))


def fused_kernel(
    senders,
    slot_ids,
    row_range,
    bad_bands,
    kernel_choice,
    flux_scale,
    range_table,
    band_table,
    vert_taps,
    horiz_taps,
    exposures,
    kept_out,
    used_out,
    pixels,
    taps,
    vertical_bank,
    horizontal_bank,
    columns_done,
    planes,
    extremes,
    totals,
    got_extremes,
    got_totals,
    load_sem,
    halo_send,
    halo_recv,
    ext_send,
    ext_recv,
    tot_send,
    tot_recv,
):
    slots, row_dev, columns = exposures.shape
    exposures_total = flux_scale.shape[0]
    kernels = vertical_bank.shape[0]
    bands = columns // BAND_COLS
    margin = TAPS // 2
    rows_out = row_dev // senders
    steps = senders.bit_length() - 1
    place = lax.axis_index("expo")
    sky = lax.axis_index("sky")

    for slot in range(slots):
        pltpu.make_async_copy(
            exposures.at[slot], pixels.at[slot, pl.ds(0, row_dev)], load_sem.at[slot]
        ).start()

    barrier = pltpu.get_barrier_semaphore()
    pl.semaphore_signal(barrier, 1, device_id={"sky": 1 - sky})
    for bit in range(steps):
        pl.semaphore_signal(barrier, 1, device_id={"expo": flip_bit(place, bit)})
    pl.semaphore_wait(barrier, steps + 1)

    edge = pl.multiple_of((1 - sky) * (row_dev - HALO), HALO)
    halo = pltpu.make_async_remote_copy(
        src_ref=exposures.at[:, pl.ds(edge, HALO)],
        dst_ref=pixels.at[:, pl.ds(row_dev, HALO)],
        send_sem=halo_send,
        recv_sem=halo_recv,
        device_id={"sky": 1 - sky},
    )
    halo.start()

    near = (
        jnp.abs(
            lax.broadcasted_iota(jnp.int32, (LANES, LANES), 0)
            - lax.broadcasted_iota(jnp.int32, (LANES, LANES), 1)
        )
        <= margin
    )

    taps[...] = jnp.zeros_like(taps)
    taps[0, 0:kernels, 0:TAPS] = vert_taps[...].astype(jnp.float32)
    taps[1, 0:kernels, 0:TAPS] = horiz_taps[...].astype(jnp.float32)
    for side in range(2):
        taps[side] = pltpu.roll(taps[side], LANES - margin % 8, 1)

    @pl.loop(0, kernels)
    def _(k):
        def circulant(side):
            spread = jnp.broadcast_to(taps[side, pl.ds(k, 1), :], (LANES, LANES))
            return pltpu.roll(spread, LANES - margin + margin % 8, 1, stride=1, stride_axis=0)

        vertical = circulant(0)
        outer = jnp.where(near, 0.0, vertical)
        outer = jnp.where(sky == 0, outer, pltpu.roll(outer, HALO, 1))
        vertical_bank[k, :, 0:LANES] = jnp.where(near, vertical, 0.0).astype(jnp.bfloat16)
        vertical_bank[k, :, LANES : LANES + HALO] = outer[:, :HALO].astype(jnp.bfloat16)
        horizontal = circulant(1).T
        horizontal_bank[k, 0:LANES, :] = jnp.where(near, horizontal, 0.0).astype(jnp.bfloat16)
        horizontal_bank[k, LANES : 2 * LANES, :] = jnp.where(near, 0.0, horizontal).astype(
            jnp.bfloat16
        )

    row_place = lax.broadcasted_iota(jnp.int32, (row_dev, LANES), 0) + sky * row_dev
    from_right = lax.broadcasted_iota(jnp.int32, (row_dev, LANES), 1) < LANES // 2

    halo.wait_recv()
    for slot in range(slots):
        pltpu.make_async_copy(
            exposures.at[slot], pixels.at[slot, pl.ds(0, row_dev)], load_sem.at[slot]
        ).wait()

    def entry_of(slot):
        return jnp.minimum(slot_ids[place, slot], exposures_total - 1)

    def filter_rows(slot, band):
        done = jnp.dot(
            vertical_bank[kernel_choice[band, entry_of(slot)]],
            pixels[slot, :, band * LANES : (band + 1) * LANES],
            preferred_element_type=jnp.float32,
        ).astype(jnp.bfloat16)
        columns_done[band, slot] = done
        return done

    def filter_band(band):
        @pl.loop(0, slots // UNROLL)
        def _(group):
            members = [group * UNROLL + i for i in range(UNROLL)]
            if band == 0:
                middle = [filter_rows(slot, 0) for slot in members]
            else:
                middle = [columns_done[band, slot] for slot in members]
            if band + 1 < bands:
                right = [filter_rows(slot, band + 1) for slot in members]
            for i, slot in enumerate(members):
                side = jnp.zeros((row_dev, LANES), jnp.float32)
                left = columns_done[band - 1, slot].astype(jnp.float32) if band else side
                side = right[i].astype(jnp.float32) if band + 1 < bands else side
                outer = jnp.where(from_right, side, left).astype(jnp.bfloat16)
                number = slot_ids[place, slot]
                entry = entry_of(slot)
                filtered = jnp.dot(
                    jnp.concatenate([middle[i], outer], axis=1),
                    horizontal_bank[kernel_choice[band, entry]],
                    preferred_element_type=jnp.float32,
                )
                open_band = (number < exposures_total) & (bad_bands[band, entry] == 0)
                last_row = jnp.where(open_band, row_range[1, entry], 0)
                usable = (row_place >= row_range[0, entry]) & (row_place < last_row)
                shown = jnp.where(usable, filtered * flux_scale[entry], -FILL)
                planes[slot] = shown.astype(jnp.bfloat16).reshape(senders, rows_out, LANES)

    def reduce_block(band, block):
        empty = jnp.asarray(-FILL, jnp.bfloat16)
        high = low = None
        total = jnp.zeros((rows_out, LANES), jnp.float32)
        for group in range(slots // 4):
            upper = [planes[4 * group + i, block] for i in range(4)]
            lower = []
            for i in range(4):
                gone = upper[i] == empty
                lower.append(jnp.where(gone, -empty, upper[i]))
                total += jnp.where(gone, jnp.zeros((), jnp.bfloat16), upper[i]).astype(jnp.float32)
            exchange(upper, SORT_FOUR, jnp.maximum, jnp.minimum)
            exchange(lower, SORT_FOUR, jnp.minimum, jnp.maximum)
            high = merge_four(high, upper, jnp.maximum, jnp.minimum) if group else upper
            low = merge_four(low, lower, jnp.minimum, jnp.maximum) if group else lower
        for i in range(4):
            extremes[band, block, i] = high[i]
            extremes[band, block, 4 + i] = low[i]
        totals[band, block] = total

    slot_of = {}
    for bit in range(steps):
        for mask in range(0, senders, 2 << bit):
            slot_of[bit, mask] = len(slot_of)

    def copies(band, mask):
        order = bit_order(band, steps)
        level = low_bit(mask, steps)
        block = flip_mask(place, mask, order)
        landing = slot_of[level, mask ^ (1 << level)]
        target = {"expo": flip_bit(place, order[level])}
        return (
            pltpu.make_async_remote_copy(
                src_ref=extremes.at[band, block],
                dst_ref=got_extremes.at[band, landing],
                send_sem=ext_send.at[band, landing],
                recv_sem=ext_recv.at[band, landing],
                device_id=target,
            ),
            pltpu.make_async_remote_copy(
                src_ref=totals.at[band, block],
                dst_ref=got_totals.at[band, landing],
                send_sem=tot_send.at[band, landing],
                recv_sem=tot_recv.at[band, landing],
                device_id=target,
            ),
        )

    started = []

    def send(band, mask):
        for copy in copies(band, mask):
            copy.start()
            started.append(copy)

    def start_band(band):
        filter_band(band)
        for mask in multiples(0, steps):
            reduce_block(band, flip_mask(place, mask, bit_order(band, steps)))
            if mask % 2:
                send(band, mask)

    def forward(band, level):
        for mask in multiples(level, steps):
            for copy in copies(band, mask ^ (1 << (level - 1))):
                copy.wait_recv()
            landing = slot_of[level - 1, mask]
            block = flip_mask(place, mask, bit_order(band, steps))
            mine = [extremes[band, block, i] for i in range(8)]
            theirs = [got_extremes[band, landing, i] for i in range(8)]
            ordered = level < steps
            high = merge_four(mine[:4], theirs[:4], jnp.maximum, jnp.minimum, ordered)
            low = merge_four(mine[4:], theirs[4:], jnp.minimum, jnp.maximum, ordered)
            total = totals[band, block] + got_totals[band, landing]
            if level == steps:
                finish(band, high, low, total)
                continue
            for i in range(4):
                extremes[band, block, i] = high[i]
                extremes[band, block, 4 + i] = low[i]
            totals[band, block] = total
            if low_bit(mask, steps) == level:
                send(band, mask)

    first_out = sky * row_dev + place * rows_out

    def finish(band, high, low, total):
        cols = slice(band * LANES, (band + 1) * LANES)
        out_place = lax.broadcasted_iota(jnp.int32, (rows_out, exposures_total), 0) + first_out
        covered = (out_place >= range_table[0:1, :]) & (out_place < range_table[1:2, :])
        clean = jnp.where(band_table[band : band + 1, :] == 0, 1.0, 0.0)
        count = lax.dot_general(
            jnp.where(covered, 1.0, 0.0).astype(jnp.bfloat16),
            jnp.broadcast_to(clean, (LANES, exposures_total)).astype(jnp.bfloat16),
            (((1,), (1,)), ((), ())),
            preferred_element_type=jnp.float32,
        )
        outer = sum(entry.astype(jnp.float32) for entry in high) + sum(
            entry.astype(jnp.float32) for entry in low
        )
        clipped = count >= MIN_VALID
        kept_out[0, :, cols] = jnp.where(clipped, total - outer, total)
        used_out[0, :, cols] = jnp.where(clipped, count - 2 * REJECT, count)

    for turn in range(bands + steps):
        if turn < bands:
            start_band(turn)
        for level in range(1, steps + 1):
            if 0 <= turn - level < bands:
                forward(turn - level, level)

    halo.wait_send()
    for copy in started:
        copy.wait_send()


def fused_shards(
    exposures, slot_ids, row_range, bad_bands, kernel_choice, flux_scale, vert_taps, horiz_taps
):
    slots, row_dev, columns = exposures.shape
    senders = lax.axis_size("expo")
    kernels = vert_taps.shape[0]
    rows_out = row_dev // senders
    smem = pl.BlockSpec(memory_space=pltpu.SMEM)
    vmem = pl.BlockSpec(memory_space=pltpu.VMEM)
    landings = senders - 1
    bands = columns // LANES
    kept, used = pl.pallas_call(
        functools.partial(fused_kernel, senders),
        out_shape=(
            jax.ShapeDtypeStruct((1, rows_out, columns), jnp.float32),
            jax.ShapeDtypeStruct((1, rows_out, columns), jnp.float32),
        ),
        in_specs=[smem] * 5 + [vmem] * 4 + [pl.BlockSpec(memory_space=pl.ANY)],
        out_specs=(vmem, vmem),
        scratch_shapes=[
            pltpu.VMEM((slots, row_dev + HALO, columns), jnp.bfloat16),
            pltpu.VMEM((2, -(-kernels // 8) * 8, LANES), jnp.float32),
            pltpu.VMEM((kernels, LANES, LANES + HALO), jnp.bfloat16),
            pltpu.VMEM((kernels, 2 * LANES, LANES), jnp.bfloat16),
            pltpu.VMEM((bands, slots, row_dev, LANES), jnp.bfloat16),
            pltpu.VMEM((slots, senders, rows_out, LANES), jnp.bfloat16),
            pltpu.VMEM((bands, senders, 8, rows_out, LANES), jnp.bfloat16),
            pltpu.VMEM((bands, senders, rows_out, LANES), jnp.float32),
            pltpu.VMEM((bands, landings, 8, rows_out, LANES), jnp.bfloat16),
            pltpu.VMEM((bands, landings, rows_out, LANES), jnp.float32),
            pltpu.SemaphoreType.DMA((slots,)),
            pltpu.SemaphoreType.DMA,
            pltpu.SemaphoreType.DMA,
            pltpu.SemaphoreType.DMA((bands, landings)),
            pltpu.SemaphoreType.DMA((bands, landings)),
            pltpu.SemaphoreType.DMA((bands, landings)),
            pltpu.SemaphoreType.DMA((bands, landings)),
        ],
        compiler_params=pltpu.CompilerParams(collective_id=0, has_side_effects=True),
    )(
        slot_ids,
        row_range.T,
        bad_bands.T,
        kernel_choice.T,
        flux_scale,
        row_range.T,
        bad_bands.T,
        vert_taps,
        horiz_taps,
        exposures,
    )
    rejected = flux_scale.shape[0] - used.astype(jnp.int32)
    return kept / jnp.maximum(used, 1.0), rejected


def shards(
    exposures, slot_ids, row_range, bad_bands, kernel_choice, flux_scale, vert_taps, horiz_taps
):
    slots, row_dev, columns = exposures.shape
    senders = lax.axis_size("expo")
    fits = (
        lax.axis_size("sky") == 2
        and senders & (senders - 1) == 0
        and senders > 1
        and row_dev == LANES
        and row_dev % (senders * 16) == 0
        and slots % max(4, UNROLL) == 0
        and columns % LANES == 0
    )
    chosen = fused_shards if fits else general_shards
    return chosen(
        exposures, slot_ids, row_range, bad_bands, kernel_choice, flux_scale, vert_taps, horiz_taps
    )


def solution(mesh):
    in_specs = (
        P(("groups", "expo"), "sky", None),
        P("groups", None),
        P("groups", None),
        P("groups", None),
        P("groups", None),
        P("groups"),
        P("groups", None),
        P("groups", None),
    )
    out_specs = (P(("groups", "sky"), "expo", None), P(("groups", "sky"), "expo", None))
    return jax.shard_map(shards, mesh=mesh, in_specs=in_specs, out_specs=out_specs, check_vma=False)
```

profile of v0, /device:TPU:0, one launch (start us, length us, event | category | flops | bytes accessed | tf_op | source)
XLA Modules:
  0.0 38.9 jit_solution(14321522096580113724)
XLA Ops:
  0.6 35.5 %shard_map.95 = (f32[1,16,512]{2,1,0:T(8,128)}, f32[1,16,512]{2,1,0:T(8,128)}) custom-call(s32[8,24]{1,0:T(8,128)} %slot_ids.1, s32[2,128]{1,0:T(2,128)} %bitcast.5, s32[4,128]{1,0:T(4,128)} %bitcast.3, s32[4,128]{1,0:T(4,128)} %bitcast.7, f32[128]{0:T(128)} %flux_scale.1, s32[2,128]{1,0:T(2,128)} %bitcast.6, s32[4,128]{1,0:T(4,128)} %bitcast.4, ...), custom_call_target="tpu_custom_call" | custom-call | tf_op jit(solution)/shard_map/pallas_call | solution.py:517
  36.1 1.4 %maximum_divide_fusion = f32[1,16,512]{2,1,0:T(8,128)} fusion(f32[1,16,512]{2,1,0:T(8,128)} %get-tuple-element.4, f32[1,16,512]{2,1,0:T(8,128)} %get-tuple-element.5), kind=kLoop, calls=%fused_computation.1 | loop fusion | flops 16384 | bytes 98304 | tf_op jit(solution)/shard_map/div | solution.py:558
  37.5 1.4 %convert_subtract_fusion = s32[1,16,512]{2,1,0:T(8,128)} fusion(f32[1,16,512]{2,1,0:T(8,128)} %get-tuple-element.5), kind=kLoop, calls=%fused_computation | loop fusion | flops 16384 | bytes 65536 | tf_op jit(solution)/shard_map/sub | solution.py:557
where the time goes:
time: 39.2 us; the launch traced here: 38.9 us
  Pallas kernels  35.5 us (91%)
  other arithmetic  2.78 us (7%)
  between operations  0.64 us (2%)
    pallas_call x1, Pallas kernels, fused_shards(): pl.pallas_call(functools.partial(fused_kernel, senders), out_shape=(jax.S...  35.5 us
    div x1, other arithmetic, fused_shards(): return (kept / jnp.maximum(used, 1.0), rejected)  1.4 us
    sub x1, other arithmetic, fused_shards(): rejected = flux_scale.shape[0] - used.astype(jnp.int32)  1.38 us

commit v1 on v0

--- a/solution.py
+++ b/solution.py
@@ -195,7 +195,7 @@
 LANES = 128
 FILL = 2.0**100
 HALO = 16
-UNROLL = 4
+UNROLL = 8
 SORT_FOUR = ((0, 1), (2, 3), (0, 2), (1, 3), (1, 2))
 SORT_BITONIC = ((0, 2), (1, 3), (0, 1), (2, 3))
 
@@ -220,8 +220,6 @@
 
 def bit_order(band, steps):
     order = list(range(steps))
-    if steps > 1 and band % 4 == 1:
-        order[0], order[1] = order[1], order[0]
     return order
 
 
@@ -488,8 +486,9 @@
             entry.astype(jnp.float32) for entry in low
         )
         clipped = count >= MIN_VALID
-        kept_out[0, :, cols] = jnp.where(clipped, total - outer, total)
-        used_out[0, :, cols] = jnp.where(clipped, count - 2 * REJECT, count)
+        used = jnp.where(clipped, count - 2 * REJECT, count)
+        kept_out[0, :, cols] = jnp.where(clipped, total - outer, total) / jnp.maximum(used, 1.0)
+        used_out[0, :, cols] = (exposures_total - used).astype(jnp.int32)
 
     for turn in range(bands + steps):
         if turn < bands:
@@ -501,6 +500,11 @@
     halo.wait_send()
     for copy in started:
         copy.wait_send()
+
+
+def relay_kernel(kept, used, kept_out, used_out):
+    kept_out[...] = kept[...]
+    used_out[...] = used[...]
 
 
 def fused_shards(
@@ -518,7 +522,7 @@
         functools.partial(fused_kernel, senders),
         out_shape=(
             jax.ShapeDtypeStruct((1, rows_out, columns), jnp.float32),
-            jax.ShapeDtypeStruct((1, rows_out, columns), jnp.float32),
+            jax.ShapeDtypeStruct((1, rows_out, columns), jnp.int32),
         ),
         in_specs=[smem] * 5 + [vmem] * 4 + [pl.BlockSpec(memory_space=pl.ANY)],
         out_specs=(vmem, vmem),
@@ -554,8 +558,15 @@
         horiz_taps,
         exposures,
     )
-    rejected = flux_scale.shape[0] - used.astype(jnp.int32)
-    return kept / jnp.maximum(used, 1.0), rejected
+    return pl.pallas_call(
+        relay_kernel,
+        out_shape=(
+            jax.ShapeDtypeStruct(kept.shape, kept.dtype),
+            jax.ShapeDtypeStruct(used.shape, used.dtype),
+        ),
+        in_specs=[vmem] * 2,
+        out_specs=(vmem, vmem),
+    )(kept, used)
 
 
 def shards(

time: 39.2 us -> 34.6 us (0.88)
  other arithmetic: 2.78 us -> 0 us
  Pallas kernels: 35.5 us -> 33.7 us
    pallas_call x1, Pallas kernels: 35.5 us -> 32.3 us  [fused_shards(): pl.pallas_call(functools.partial(fused_kernel, senders), out_shape=(jax.S...]
    pallas_call x0 -> x1, Pallas kernels: none -> 1.4 us  [fused_shards(): pl.pallas_call(relay_kernel, out_shape=(jax.ShapeDtypeStruct(kept.shape,...]
    div x1 -> x0, other arithmetic: 1.4 us -> none  [fused_shards(): return (kept / jnp.maximum(used, 1.0), rejected)]
    sub x1 -> x0, other arithmetic: 1.38 us -> none  [fused_shards(): rejected = flux_scale.shape[0] - used.astype(jnp.int32)]
where the time goes in v1:
time: 34.6 us; the launch traced here: 34.3 us
  Pallas kernels  33.7 us (97%)
  between operations  0.64 us (2%)
    pallas_call x1, Pallas kernels, fused_shards(): pl.pallas_call(functools.partial(fused_kernel, senders), out_shape=(jax.S...  32.3 us
    pallas_call x1, Pallas kernels, fused_shards(): pl.pallas_call(relay_kernel, out_shape=(jax.ShapeDtypeStruct(kept.shape,...  1.4 us

profile of v1, /device:TPU:0, one launch (start us, length us, event | category | flops | bytes accessed | tf_op | source)
XLA Modules:
  0.0 34.3 jit_solution(10026608878364525802)
XLA Ops:
  0.6 32.3 %shard_map.95 = (f32[1,16,512]{2,1,0:T(8,128)}, s32[1,16,512]{2,1,0:T(8,128)}) custom-call(s32[8,24]{1,0:T(8,128)} %slot_ids.1, s32[2,128]{1,0:T(2,128)} %bitcast.5, s32[4,128]{1,0:T(4,128)} %bitcast.3, s32[4,128]{1,0:T(4,128)} %bitcast.7, f32[128]{0:T(128)} %flux_scale.1, s32[2,128]{1,0:T(2,128)} %bitcast.6, s32[4,128]{1,0:T(4,128)} %bitcast.4, ...), custom_call_target="tpu_custom_call" | custom-call | tf_op jit(solution)/shard_map/pallas_call | solution.py:521
  32.9 1.4 %shard_map.96 = (f32[1,16,512]{2,1,0:T(8,128)}, s32[1,16,512]{2,1,0:T(8,128)}) custom-call(f32[1,16,512]{2,1,0:T(8,128)} %get-tuple-element.4.kept, s32[1,16,512]{2,1,0:T(8,128)} %get-tuple-element.5.used), custom_call_target="tpu_custom_call" | custom-call | tf_op jit(solution)/shard_map/pallas_call | solution.py:561

commit v2 on v1

--- a/solution.py
+++ b/solution.py
@@ -195,7 +195,7 @@
 LANES = 128
 FILL = 2.0**100
 HALO = 16
-UNROLL = 8
+UNROLL = 12
 SORT_FOUR = ((0, 1), (2, 3), (0, 2), (1, 3), (1, 2))
 SORT_BITONIC = ((0, 2), (1, 3), (0, 1), (2, 3))
 
@@ -338,6 +338,7 @@
 
     row_place = lax.broadcasted_iota(jnp.int32, (row_dev, LANES), 0) + sky * row_dev
     from_right = lax.broadcasted_iota(jnp.int32, (row_dev, LANES), 1) < LANES // 2
+    from_right = jnp.where(from_right, 1.0, 0.0).astype(jnp.bfloat16)
 
     halo.wait_recv()
     for slot in range(slots):
@@ -368,10 +369,10 @@
             if band + 1 < bands:
                 right = [filter_rows(slot, band + 1) for slot in members]
             for i, slot in enumerate(members):
-                side = jnp.zeros((row_dev, LANES), jnp.float32)
-                left = columns_done[band - 1, slot].astype(jnp.float32) if band else side
-                side = right[i].astype(jnp.float32) if band + 1 < bands else side
-                outer = jnp.where(from_right, side, left).astype(jnp.bfloat16)
+                side = jnp.zeros((row_dev, LANES), jnp.bfloat16)
+                left = columns_done[band - 1, slot] if band else side
+                side = right[i] if band + 1 < bands else side
+                outer = jnp.where(from_right > 0, side, left)
                 number = slot_ids[place, slot]
                 entry = entry_of(slot)
                 filtered = jnp.dot(

time: 34.6 us -> 34.5 us (level)
  no operation moved by 1% of the time
where the time goes in v2:
time: 34.5 us; the launch traced here: 34.2 us
  Pallas kernels  33.6 us (97%)
  between operations  0.64 us (2%)
    pallas_call x1, Pallas kernels, fused_shards(): pl.pallas_call(functools.partial(fused_kernel, senders), out_shape=(jax.S...  32.2 us
    pallas_call x1, Pallas kernels, fused_shards(): pl.pallas_call(relay_kernel, out_shape=(jax.ShapeDtypeStruct(kept.shape,...  1.4 us

profile of v2, /device:TPU:0, one launch (start us, length us, event | category | flops | bytes accessed | tf_op | source)
XLA Modules:
  0.0 34.2 jit_solution(9664940494624116202)
XLA Ops:
  0.6 32.2 %shard_map.95 = (f32[1,16,512]{2,1,0:T(8,128)}, s32[1,16,512]{2,1,0:T(8,128)}) custom-call(s32[8,24]{1,0:T(8,128)} %slot_ids.1, s32[2,128]{1,0:T(2,128)} %bitcast.5, s32[4,128]{1,0:T(4,128)} %bitcast.3, s32[4,128]{1,0:T(4,128)} %bitcast.7, f32[128]{0:T(128)} %flux_scale.1, s32[2,128]{1,0:T(2,128)} %bitcast.6, s32[4,128]{1,0:T(4,128)} %bitcast.4, ...), custom_call_target="tpu_custom_call" | custom-call | tf_op jit(solution)/shard_map/pallas_call | solution.py:522
  32.8 1.4 %shard_map.96 = (f32[1,16,512]{2,1,0:T(8,128)}, s32[1,16,512]{2,1,0:T(8,128)}) custom-call(f32[1,16,512]{2,1,0:T(8,128)} %get-tuple-element.4.kept, s32[1,16,512]{2,1,0:T(8,128)} %get-tuple-element.5.used), custom_call_target="tpu_custom_call" | custom-call | tf_op jit(solution)/shard_map/pallas_call | solution.py:562
